TPU v7x, 512 devices: a whole 4x4x16 slice. The times are simulated.
512 devices in a mesh: batch: 8 (over x, core), head: 2 (over z_hi), expert: 32 (over z_lo, y).
Axes of the slice: x: 4, y: 4, z: 16 (z_hi: 2, z_lo: 8; z = z_hi * 8 + z_lo), core: 2. Of those that a mesh axis runs over, the one named last changes fastest.
Arguments:
- hidden_in: bfloat16 [65536, 2048], P(('batch', 'head', 'expert')), may hold values from -6 to 6
- norm_gain: float32 [2048], replicated, may hold values from 0.25 to 1.75
- w_gate: bfloat16 [64, 2048, 384], P('expert', ('batch', 'head')), may hold values from -0.125 to 0.125
- w_up: bfloat16 [64, 2048, 384], P('expert', ('batch', 'head')), may hold values from -0.125 to 0.125
- w_down: bfloat16 [64, 384, 2048], P('expert', None, ('batch', 'head')), may hold values from -0.3125 to 0.3125
- expert_ids: int32 [65536, 2], P(('batch', 'head', 'expert')), may hold values from 0 to 63, all different within a row; in each aligned block of 128 rows (0 to 127, 128 to 255, ...) at most 6 rows name the same one
- gate_codes: int32 [65536, 2], P(('batch', 'head', 'expert')), may hold values from 4096 to 65535
- out_grad: bfloat16 [65536, 2048], P(('batch', 'head', 'expert')), may hold values from -6 to 6
Outputs:
- output: bfloat16 [65536, 2048], P(('batch', 'head', 'expert'))
- grad_in: bfloat16 [65536, 2048], P(('batch', 'head', 'expert'))
Inputs may be any that keep to these rules, and one draw needn't show every extreme that they name: `expert_ids`: each row names 2 different experts; within the rows of one device no expert is named more than 6 times, a bound that some block reaches.
All inputs are finite; a program needn't handle non-finite values.
Results may differ from a plain program's by a relative error of at most 0.0055.
Values may be sent and summed in bfloat16 or wider, within the bound.
No kernel may reach another device: no remote copies, remote signals or barrier semaphores. Data moves between devices by JAX's collectives and lax.ppermute only.
A program may use at most 128 MiB of HBM per device.

v0:
```python
import numpy as np
import jax
import jax.numpy as jnp
from jax import lax
from jax.experimental import pallas as pl
from jax.experimental.pallas import tpu as pltpu
from jax.sharding import Mesh, PartitionSpec as P

epsilon = 1e-06
BF = jnp.bfloat16
F32 = jnp.float32
I32 = jnp.int32
VMEM = pltpu.VMEM
MIB = 1024 * 1024

X, C, H, B, A, Y = 4, 2, 2, 2, 4, 4
PEERS = X * C * Y
TOK, D, FW, CAP = 128, 2048, 384, 6
PER = 4 * CAP
ROWS = PEERS * PER
GROUPS = 4
GROUP = ROWS // GROUPS
KIND = GROUP // 4
SLOTS = GROUPS * KIND


def sort_matrix():
    natural = np.arange(GROUP)
    place = (natural % PER) // CAP * KIND + natural // PER * CAP + natural % CAP
    to_natural = np.zeros((GROUP, GROUP), np.float32)
    to_natural[natural, place] = 1.0
    return to_natural


def whole(n):
    return [pl.BlockSpec(memory_space=VMEM)] * n


def params(mib=24):
    return pltpu.CompilerParams(vmem_limit_bytes=mib * MIB)


def split_kernel(gate_ref, up_ref, down_ref, *refs):
    out_refs, sem = refs[:X], refs[X]
    x = lax.axis_index("X")
    copies = []
    for r in range(X):
        q = (x + r) & 3
        rows = pl.ds(pl.multiple_of(q * 32, 32), 32)
        for m, ref in enumerate((gate_ref, up_ref)):
            for f in range(3):
                copies.append(
                    pltpu.make_async_copy(
                        ref.at[:, rows, pl.ds(f * 128, 128)],
                        out_refs[r].at[:, m, pl.ds(f * 32, 32), :],
                        sem,
                    )
                )
        rows = pl.ds(pl.multiple_of(q * 96, 32), 96)
        copies.append(
            pltpu.make_async_copy(down_ref.at[:, rows, :], out_refs[r].at[:, 2, :, :], sem)
        )
    for copy in copies:
        copy.start()
    for copy in copies:
        copy.wait()


def split_weights(*mats):
    mats = [pltpu.with_memory_space_constraint(mat, pltpu.HBM) for mat in mats]
    return pl.pallas_call(
        split_kernel,
        out_shape=(pltpu.VMEM((2, 3, 96, 128), BF),) * X,
        in_specs=[pl.BlockSpec(memory_space=pltpu.HBM)] * 3,
        out_specs=tuple(whole(X)),
        scratch_shapes=[pltpu.SemaphoreType.DMA],
        compiler_params=params(),
        name="split_weights",
    )(*mats)


def send_home(pieces):
    moved = []
    for r in range(X):
        pairs = [(x * A + a, a * A + (x + r) % X) for x in range(X) for a in range(A)]
        moved.append(lax.ppermute(pieces[r], ("X", "A"), pairs))
    return moved


def place_kernel(*refs):
    keep_ref, give_ref, sem = refs[X:]
    a, c = lax.axis_index("A"), lax.axis_index("C")
    copies = []
    for r in range(X):
        at = (a - r) & 3
        copies.append(pltpu.make_async_copy(refs[r].at[c], keep_ref.at[at], sem))
        copies.append(pltpu.make_async_copy(refs[r].at[1 - c], give_ref.at[at], sem))
    for copy in copies:
        copy.start()
    for copy in copies:
        copy.wait()


def place(pieces):
    return pl.pallas_call(
        place_kernel,
        out_shape=(pltpu.VMEM((X, 3, 96, 128), BF),) * 2,
        in_specs=[pl.BlockSpec(memory_space=pl.ANY)] * X,
        out_specs=tuple(whole(2)),
        scratch_shapes=[pltpu.SemaphoreType.DMA],
        compiler_params=params(),
        name="place",
    )(*pieces)


Z = H * B * A
UP = [(z, (z + 1) % Z) for z in range(Z)]
DOWN = [(z, (z - 1) % Z) for z in range(Z)]


def around(halves):
    found = [[half] + [None] * (Z - 1) for half in halves]
    axes = ("H", "B", "A")
    for k in range(1, Z // 2 + 1):
        for i in range(2):
            found[i][k] = lax.ppermute(found[i][k - 1], axes, UP)
            if k < Z // 2:
                found[i][Z - k] = lax.ppermute(found[i][(Z - k + 1) % Z], axes, DOWN)
    return [pltpu.with_memory_space_constraint(f, pltpu.HBM) for f in found[0] + found[1]]


def route_rows(ids0, ids1):
    labels = lax.broadcasted_iota(I32, (64, TOK), 0)
    m0, m1 = labels == ids0, labels == ids1
    one, zero = jnp.ones((64, TOK), F32), jnp.zeros((64, TOK), F32)
    both = (jnp.where(m0, one, zero) + jnp.where(m1, one, zero)).astype(BF)
    earlier = jnp.where(
        lax.broadcasted_iota(I32, (TOK, TOK), 0) < lax.broadcasted_iota(I32, (TOK, TOK), 1),
        jnp.ones((TOK, TOK), F32),
        jnp.zeros((TOK, TOK), F32),
    ).astype(BF)
    before = jnp.dot(both, earlier, preferred_element_type=F32)

    def row(ids, mask):
        position = jnp.sum(jnp.where(mask, before, zero), axis=0, keepdims=True).astype(I32)
        x, b = (ids >> 3) & 3, ids >> 5
        y, c = (ids >> 1) & 3, ids & 1
        return ((x * C + c) * Y + y) * PER + b * CAP + position

    return row(ids0, m0), row(ids1, m1)


def row_scale_of(hidden):
    return lax.rsqrt(jnp.mean(hidden * hidden, axis=1, keepdims=True) + epsilon)


def dispatch_kernel(ids_ref, hidden_ref, gain_ref, grad_ref, out_ref):
    hidden = hidden_ref[...].astype(F32)
    normed = (hidden * row_scale_of(hidden) * gain_ref[...]).astype(BF)
    both = jnp.concatenate([normed, grad_ref[...]], axis=0)
    r0, r1 = route_rows(ids_ref[0:1, :], ids_ref[1:2, :])
    one, zero = jnp.ones((GROUP, TOK), F32), jnp.zeros((GROUP, TOK), F32)
    for g in range(GROUPS):
        at = lax.broadcasted_iota(I32, (GROUP, TOK), 0) + g * GROUP
        picks = []
        for shift in (0, 2 * CAP):
            hit = (at == r0 + shift) | (at == r1 + shift)
            picks.append(jnp.where(hit, one, zero).astype(BF))
        chosen = jnp.concatenate(picks, axis=1)
        out_ref[g * GROUP : (g + 1) * GROUP, :] = jnp.dot(
            chosen, both, preferred_element_type=F32
        ).astype(BF)


def dispatch(ids, hidden, gain, grad):
    return pl.pallas_call(
        dispatch_kernel,
        out_shape=pltpu.VMEM((ROWS, D), BF),
        in_specs=whole(4),
        out_specs=pl.BlockSpec(memory_space=VMEM),
        compiler_params=params(),
        name="dispatch",
    )(ids, hidden, gain, grad)


def lanes(n):
    c, x = n // X, n % X
    return (x * C + c) * 256


def sort_kernel(to_sorted_ref, rows_ref, out_ref):
    for g in range(GROUPS):
        block = jnp.dot(
            to_sorted_ref[...],
            rows_ref[g * GROUP : (g + 1) * GROUP, :],
            preferred_element_type=F32,
        ).astype(BF)
        for k in range(4):
            for n in range(8):
                at = lanes(n)
                out_ref[k, g * KIND : (g + 1) * KIND, n * 256 : (n + 1) * 256] = block[
                    k * KIND : (k + 1) * KIND, at : at + 256
                ]


def sort_rows(to_sorted, rows):
    return pl.pallas_call(
        sort_kernel,
        out_shape=pltpu.VMEM((4, SLOTS, D), BF),
        in_specs=whole(2),
        out_specs=pl.BlockSpec(memory_space=VMEM),
        compiler_params=params(),
        name="sort_rows",
    )(to_sorted, rows)


def expert_kernel(rows_ref, to_natural_ref, *refs):
    pieces, (out_ref, in_mats, down_mat, sem) = refs[: 2 * Z], refs[2 * Z :]
    me = (lax.axis_index("H") * B + lax.axis_index("B")) * A + lax.axis_index("A")
    core = lax.axis_index("C")
    copies = []
    for i in range(2):
        c = core if i == 0 else 1 - core
        for k in range(Z):
            z = (me - k) & (Z - 1)
            h, b, q = z >> 3, (z >> 2) & 1, z & 3
            ref = pieces[i * Z + k]
            for m in range(2):
                for f in range(3):
                    copies.append(
                        pltpu.make_async_copy(
                            ref.at[:, m, pl.ds(f * 32, 32), :],
                            in_mats.at[b, m, c, :, h, q, :, pl.ds(f * 128, 128)],
                            sem,
                        )
                    )
            copies.append(pltpu.make_async_copy(ref.at[:, 2], down_mat.at[b, c, :, h, q], sem))
    for copy in copies:
        copy.start()
    for copy in copies:
        copy.wait()

    def down_chunk(b, k):
        c, x = k // X, k % X
        return jnp.concatenate(
            [down_mat[b, c, x, h].reshape(FW, 128) for h in range(H)], axis=1
        )

    inner, d_gate, d_up = [], [], []
    for b in range(B):
        rows = rows_ref[b]
        gate_pre = jnp.dot(rows, in_mats[b, 0].reshape(D, FW), preferred_element_type=F32)
        up_pre = jnp.dot(rows, in_mats[b, 1].reshape(D, FW), preferred_element_type=F32)
        back = jnp.zeros((SLOTS, FW), F32)
        for k in range(8):
            chunk = down_chunk(b, k)
            back = back + lax.dot_general(
                rows_ref[2 + b, :, k * 256 : (k + 1) * 256],
                chunk,
                (((1,), (1,)), ((), ())),
                preferred_element_type=F32,
            )
        s = jax.nn.sigmoid(gate_pre)
        silu = gate_pre * s
        inner.append((silu * up_pre).astype(BF))
        d_gate.append((back * up_pre * s * (1.0 + gate_pre * (1.0 - s))).astype(BF))
        d_up.append((back * silu).astype(BF))
    for k in range(8):
        parts = []
        for b in range(B):
            chunk = down_chunk(b, k)
            parts.append(jnp.dot(inner[b], chunk, preferred_element_type=F32).astype(BF))
        for b in range(B):
            total = lax.dot_general(
                d_gate[b],
                in_mats[b, 0, k // X, k % X].reshape(256, FW),
                (((1,), (1,)), ((), ())),
                preferred_element_type=F32,
            ) + lax.dot_general(
                d_up[b],
                in_mats[b, 1, k // X, k % X].reshape(256, FW),
                (((1,), (1,)), ((), ())),
                preferred_element_type=F32,
            )
            parts.append(total.astype(BF))
        for g in range(GROUPS):
            block = jnp.concatenate([p[g * KIND : (g + 1) * KIND] for p in parts], axis=0)
            out_ref[g * GROUP : (g + 1) * GROUP, lanes(k) : lanes(k) + 256] = jnp.dot(
                to_natural_ref[...], block, preferred_element_type=F32
            ).astype(BF)


def experts(rows, to_natural, weights):
    return pl.pallas_call(
        expert_kernel,
        out_shape=pltpu.VMEM((ROWS, D), BF),
        in_specs=whole(2) + [pl.BlockSpec(memory_space=pl.ANY)] * (2 * Z),
        out_specs=pl.BlockSpec(memory_space=VMEM),
        scratch_shapes=[
            VMEM((B, 2, C, X, H, A, 32, FW), BF),
            VMEM((B, C, X, H, A, 96, 128), BF),
            pltpu.SemaphoreType.DMA,
        ],
        compiler_params=params(36),
        name="experts",
    )(rows, to_natural, *weights)


def combine_kernel(ids_ref, codes_ref, ret_ref, hidden_ref, gain_ref, grad_ref, out_ref, gin_ref):
    r0, r1 = route_rows(ids_ref[0:1, :], ids_ref[1:2, :])
    codes = codes_ref[...].astype(F32)
    weights = codes / (codes[0:1, :] + codes[1:2, :])
    lines = jnp.concatenate(
        [r0.astype(F32), r1.astype(F32), weights, jnp.zeros((TOK - 4, TOK), F32)], axis=0
    )
    columns = jnp.transpose(lines)
    c0, c1 = columns[:, 0:1].astype(I32), columns[:, 1:2].astype(I32)
    w0, w1 = columns[:, 2:3], columns[:, 3:4]
    at = lax.broadcasted_iota(I32, (TOK, ROWS), 1)
    one, zero = jnp.ones((TOK, ROWS), F32), jnp.zeros((TOK, ROWS), F32)
    chosen = jnp.concatenate(
        [
            jnp.where(at == c + shift, one, zero).astype(BF)
            for shift in (0, 2 * CAP)
            for c in (c0, c1)
        ],
        axis=0,
    )
    picked = jnp.dot(chosen, ret_ref[...], preferred_element_type=F32)
    mixture = picked[0:TOK] * w0 + picked[TOK : 2 * TOK] * w1
    grad_normed = picked[2 * TOK : 3 * TOK] * w0 + picked[3 * TOK :] * w1
    hidden = hidden_ref[...].astype(F32)
    row_scale = row_scale_of(hidden)
    out_ref[...] = (hidden + mixture).astype(BF)
    scaled = gain_ref[...] * grad_normed
    inner_mean = jnp.mean(scaled * hidden, axis=1, keepdims=True)
    gin_ref[...] = (
        grad_ref[...].astype(F32)
        + row_scale * scaled
        - hidden * ((row_scale * row_scale * row_scale) * inner_mean)
    ).astype(BF)


def combine(ids, codes, returned, hidden, gain, grad):
    shape = jax.ShapeDtypeStruct((TOK, D), BF)
    return pl.pallas_call(
        combine_kernel,
        out_shape=(shape, shape),
        in_specs=whole(6),
        out_specs=tuple(whole(2)),
        compiler_params=params(),
        name="combine",
    )(ids, codes, returned, hidden, gain, grad)


def exchange(rows):
    blocks = rows.reshape(PEERS, PER, D)
    return lax.all_to_all(blocks, ("X", "C", "Y"), 0, 0, tiled=True).reshape(ROWS, D)


def body(hidden_in, norm_gain, w_gate, w_up, w_down, expert_ids, gate_codes, out_grad):
    gain = norm_gain.reshape(1, D)
    ids, codes = expert_ids.T, gate_codes.T
    to_natural = sort_matrix()
    keep, give = place(send_home(split_weights(w_gate, w_up, w_down)))
    weights = around((keep, lax.ppermute(give, "C", [(0, 1), (1, 0)])))
    sent = dispatch(ids, hidden_in, gain, out_grad)
    arrived = exchange(sent)
    rows = sort_rows(jnp.asarray(to_natural.T, BF), arrived)
    rows = pltpu.with_memory_space_constraint(rows, VMEM)
    results = experts(rows, jnp.asarray(to_natural, BF), weights)
    returned = exchange(results)
    return combine(ids, codes, returned, hidden_in, gain, out_grad)


def solution(mesh):
    fine = Mesh(mesh.devices.reshape(X, C, H, B, A, Y), ("X", "C", "H", "B", "A", "Y"))
    tokens = P(("X", "C", "H", "B", "A", "Y"), None)
    owner, feature = ("B", "A", "Y"), ("X", "C", "H")
    in_specs = (
        tokens,
        P(),
        P(owner, feature, None),
        P(owner, feature, None),
        P(owner, None, feature),
        tokens,
        tokens,
        tokens,
    )
    return jax.shard_map(
        body, mesh=fine, in_specs=in_specs, out_specs=(tokens, tokens), check_vma=False
    )
```

profile of v0, /device:TPU:1, one launch (start us, length us, event | category | flops | bytes accessed | tf_op | source)
XLA Modules:
  0.0 249.0 jit_solution(8465796078219920927)
XLA Ops:
  6.9 10.7 %all-to-all-start = ((bf16[32,24,2048]{2,1,0:T(8,128)(2,1)}), bf16[32,24,2048]{2,1,0:T(8,128)(2,1)S(1)}, u32[]{:S(2)}, u32[]{:S(2)}) async-start(bf16[32,24,2048]{2,1,0:T(8,128)(2,1)} %bitcast.8), calls=%async_computation | async-start | bytes 6291456 | tf_op jit(solution)/shard_map/all_to_all | solution.py:358
  19.5 5.7 %collective-permute-start.1 = (bf16[2,3,96,128]{3,2,1,0:T(8,128)(2,1)S(1)}, bf16[2,3,96,128]{3,2,1,0:T(8,128)(2,1)S(1)}, u32[]{:S(2)}, u32[]{:S(2)}) collective-permute-start(bf16[2,3,96,128]{3,2,1,0:T(8,128)(2,1)S(1)} %get-tuple-element.9), channel_id=1, source_target_pairs={{0,4},{4,132},{8,260},{12,388},{128,8},{132,136},{136,264},{140,39... | collective-permute-start | bytes 442376 | tf_op jit(solution)/shard_map/ppermute | solution.py:86
  25.2 4.4 %collective-permute-start.2 = (bf16[2,3,96,128]{3,2,1,0:T(8,128)(2,1)S(1)}, bf16[2,3,96,128]{3,2,1,0:T(8,128)(2,1)S(1)}, u32[]{:S(2)}, u32[]{:S(2)}) collective-permute-start(bf16[2,3,96,128]{3,2,1,0:T(8,128)(2,1)S(1)} %get-tuple-element.10), channel_id=1, source_target_pairs={{0,8},{4,136},{8,264},{12,392},{128,12},{132,140},{136,268},{140,3... | collective-permute-start | bytes 442376 | tf_op jit(solution)/shard_map/ppermute | solution.py:86
  29.6 4.8 %collective-permute-start.3 = (bf16[2,3,96,128]{3,2,1,0:T(8,128)(2,1)S(1)}, bf16[2,3,96,128]{3,2,1,0:T(8,128)(2,1)S(1)}, u32[]{:S(2)}, u32[]{:S(2)}) collective-permute-start(bf16[2,3,96,128]{3,2,1,0:T(8,128)(2,1)S(1)} %get-tuple-element.11), channel_id=1, source_target_pairs={{0,12},{4,140},{8,268},{12,396},{128,0},{132,128},{136,256},{140,3... | collective-permute-start | bytes 442376 | tf_op jit(solution)/shard_map/ppermute | solution.py:86
  34.4 20.6 %collective-permute-done.1.refs_1_ = bf16[2,3,96,128]{3,2,1,0:T(8,128)(2,1)S(1)} collective-permute-done((bf16[2,3,96,128]{3,2,1,0:T(8,128)(2,1)S(1)}, bf16[2,3,96,128]{3,2,1,0:T(8,128)(2,1)S(1)}, u32[]{:S(2)}, u32[]{:S(2)}) %collective-permute-start.1) | collective-permute-done | bytes 147488 | tf_op jit(solution)/shard_map/ppermute | solution.py:86
  54.9 6.6 %collective-permute-done.2.refs_2_ = bf16[2,3,96,128]{3,2,1,0:T(8,128)(2,1)S(1)} collective-permute-done((bf16[2,3,96,128]{3,2,1,0:T(8,128)(2,1)S(1)}, bf16[2,3,96,128]{3,2,1,0:T(8,128)(2,1)S(1)}, u32[]{:S(2)}, u32[]{:S(2)}) %collective-permute-start.2) | collective-permute-done | bytes 147488 | tf_op jit(solution)/shard_map/ppermute | solution.py:86
  69.5 4.6 %collective-permute-start.12 = (bf16[4,3,96,128]{3,2,1,0:T(8,128)(2,1)S(1)}, bf16[4,3,96,128]{3,2,1,0:T(8,128)(2,1)S(1)}, u32[]{:S(2)}, u32[]{:S(2)}) collective-permute-start(bf16[4,3,96,128]{3,2,1,0:T(8,128)(2,1)S(1)} %get-tuple-element.12.refs_0_), channel_id=1, source_target_pairs={{0,60},{4,0},{8,4},{12,8},{16,12},{20,16},{24,20},{28,24},{32,28},... | collective-permute-start | bytes 884744 | tf_op jit(solution)/shard_map/ppermute | solution.py:128
  74.1 3.2 %collective-permute-done.4.refs_1_ = bf16[4,3,96,128]{3,2,1,0:T(8,128)(2,1)S(1)} collective-permute-done((bf16[4,3,96,128]{3,2,1,0:T(8,128)(2,1)S(1)}, bf16[4,3,96,128]{3,2,1,0:T(8,128)(2,1)S(1)}, u32[]{:S(2)}, u32[]{:S(2)}) %collective-permute-start.4) | collective-permute-done | bytes 294944 | tf_op jit(solution)/shard_map/ppermute | solution.py:126
  79.2 4.6 %collective-permute-start.28 = (bf16[4,3,96,128]{3,2,1,0:T(8,128)(2,1)S(1)}, bf16[4,3,96,128]{3,2,1,0:T(8,128)(2,1)S(1)}, u32[]{:S(2)}, u32[]{:S(2)}) collective-permute-start(bf16[4,3,96,128]{3,2,1,0:T(8,128)(2,1)S(1)} %collective-permute-done.19.refs_16_), channel_id=1, source_target_pairs={{0,60},{4,0},{8,4},{12,8},{16,12},{20,16},{24,20},{28,24},{32,28},... | collective-permute-start | bytes 884744 | tf_op jit(solution)/shard_map/ppermute | solution.py:128
  85.7 4.6 %collective-permute-start.13 = (bf16[4,3,96,128]{3,2,1,0:T(8,128)(2,1)S(1)}, bf16[4,3,96,128]{3,2,1,0:T(8,128)(2,1)S(1)}, u32[]{:S(2)}, u32[]{:S(2)}) collective-permute-start(bf16[4,3,96,128]{3,2,1,0:T(8,128)(2,1)S(1)} %collective-permute-done.12.refs_15_), channel_id=1, source_target_pairs={{0,60},{4,0},{8,4},{12,8},{16,12},{20,16},{24,20},{28,24},{32,28},... | collective-permute-start | bytes 884744 | tf_op jit(solution)/shard_map/ppermute | solution.py:128
  92.3 4.6 %collective-permute-start.29 = (bf16[4,3,96,128]{3,2,1,0:T(8,128)(2,1)S(1)}, bf16[4,3,96,128]{3,2,1,0:T(8,128)(2,1)S(1)}, u32[]{:S(2)}, u32[]{:S(2)}) collective-permute-start(bf16[4,3,96,128]{3,2,1,0:T(8,128)(2,1)S(1)} %collective-permute-done.28.refs_31_), channel_id=1, source_target_pairs={{0,60},{4,0},{8,4},{12,8},{16,12},{20,16},{24,20},{28,24},{32,28},... | collective-permute-start | bytes 884744 | tf_op jit(solution)/shard_map/ppermute | solution.py:128
  98.8 4.6 %collective-permute-start.14 = (bf16[4,3,96,128]{3,2,1,0:T(8,128)(2,1)S(1)}, bf16[4,3,96,128]{3,2,1,0:T(8,128)(2,1)S(1)}, u32[]{:S(2)}, u32[]{:S(2)}) collective-permute-start(bf16[4,3,96,128]{3,2,1,0:T(8,128)(2,1)S(1)} %collective-permute-done.13.refs_14_), channel_id=1, source_target_pairs={{0,60},{4,0},{8,4},{12,8},{16,12},{20,16},{24,20},{28,24},{32,28},... | collective-permute-start | bytes 884744 | tf_op jit(solution)/shard_map/ppermute | solution.py:128
  105.4 4.6 %collective-permute-start.30 = (bf16[4,3,96,128]{3,2,1,0:T(8,128)(2,1)S(1)}, bf16[4,3,96,128]{3,2,1,0:T(8,128)(2,1)S(1)}, u32[]{:S(2)}, u32[]{:S(2)}) collective-permute-start(bf16[4,3,96,128]{3,2,1,0:T(8,128)(2,1)S(1)} %collective-permute-done.29.refs_30_), channel_id=1, source_target_pairs={{0,60},{4,0},{8,4},{12,8},{16,12},{20,16},{24,20},{28,24},{32,28},... | collective-permute-start | bytes 884744 | tf_op jit(solution)/shard_map/ppermute | solution.py:128
  111.9 4.6 %collective-permute-start.15 = (bf16[4,3,96,128]{3,2,1,0:T(8,128)(2,1)S(1)}, bf16[4,3,96,128]{3,2,1,0:T(8,128)(2,1)S(1)}, u32[]{:S(2)}, u32[]{:S(2)}) collective-permute-start(bf16[4,3,96,128]{3,2,1,0:T(8,128)(2,1)S(1)} %collective-permute-done.14.refs_13_), channel_id=1, source_target_pairs={{0,60},{4,0},{8,4},{12,8},{16,12},{20,16},{24,20},{28,24},{32,28},... | collective-permute-start | bytes 884744 | tf_op jit(solution)/shard_map/ppermute | solution.py:128
  118.5 4.6 %collective-permute-start.31 = (bf16[4,3,96,128]{3,2,1,0:T(8,128)(2,1)S(1)}, bf16[4,3,96,128]{3,2,1,0:T(8,128)(2,1)S(1)}, u32[]{:S(2)}, u32[]{:S(2)}) collective-permute-start(bf16[4,3,96,128]{3,2,1,0:T(8,128)(2,1)S(1)} %collective-permute-done.30.refs_29_), channel_id=1, source_target_pairs={{0,60},{4,0},{8,4},{12,8},{16,12},{20,16},{24,20},{28,24},{32,28},... | collective-permute-start | bytes 884744 | tf_op jit(solution)/shard_map/ppermute | solution.py:128
  125.0 4.6 %collective-permute-start.16 = (bf16[4,3,96,128]{3,2,1,0:T(8,128)(2,1)S(1)}, bf16[4,3,96,128]{3,2,1,0:T(8,128)(2,1)S(1)}, u32[]{:S(2)}, u32[]{:S(2)}) collective-permute-start(bf16[4,3,96,128]{3,2,1,0:T(8,128)(2,1)S(1)} %collective-permute-done.15.refs_12_), channel_id=1, source_target_pairs={{0,60},{4,0},{8,4},{12,8},{16,12},{20,16},{24,20},{28,24},{32,28},... | collective-permute-start | bytes 884744 | tf_op jit(solution)/shard_map/ppermute | solution.py:128
  131.6 4.6 %collective-permute-start.32 = (bf16[4,3,96,128]{3,2,1,0:T(8,128)(2,1)S(1)}, bf16[4,3,96,128]{3,2,1,0:T(8,128)(2,1)S(1)}, u32[]{:S(2)}, u32[]{:S(2)}) collective-permute-start(bf16[4,3,96,128]{3,2,1,0:T(8,128)(2,1)S(1)} %collective-permute-done.31.refs_28_), channel_id=1, source_target_pairs={{0,60},{4,0},{8,4},{12,8},{16,12},{20,16},{24,20},{28,24},{32,28},... | collective-permute-start | bytes 884744 | tf_op jit(solution)/shard_map/ppermute | solution.py:128
  138.1 4.6 %collective-permute-start.17 = (bf16[4,3,96,128]{3,2,1,0:T(8,128)(2,1)S(1)}, bf16[4,3,96,128]{3,2,1,0:T(8,128)(2,1)}, u32[]{:S(2)}, u32[]{:S(2)}) collective-permute-start(bf16[4,3,96,128]{3,2,1,0:T(8,128)(2,1)S(1)} %collective-permute-done.16.refs_11_), channel_id=1, source_target_pairs={{0,60},{4,0},{8,4},{12,8},{16,12},{20,16},{24,20},{28,24},{32,28},... | collective-permute-start | bytes 884744 | tf_op jit(solution)/shard_map/ppermute | solution.py:128
  144.7 4.6 %collective-permute-start.33 = (bf16[4,3,96,128]{3,2,1,0:T(8,128)(2,1)S(1)}, bf16[4,3,96,128]{3,2,1,0:T(8,128)(2,1)}, u32[]{:S(2)}, u32[]{:S(2)}) collective-permute-start(bf16[4,3,96,128]{3,2,1,0:T(8,128)(2,1)S(1)} %collective-permute-done.32.refs_27_), channel_id=1, source_target_pairs={{0,60},{4,0},{8,4},{12,8},{16,12},{20,16},{24,20},{28,24},{32,28},... | collective-permute-start | bytes 884744 | tf_op jit(solution)/shard_map/ppermute | solution.py:128
  151.2 4.6 %collective-permute-start.18 = (bf16[4,3,96,128]{3,2,1,0:T(8,128)(2,1)}, bf16[4,3,96,128]{3,2,1,0:T(8,128)(2,1)}, u32[]{:S(2)}, u32[]{:S(2)}) collective-permute-start(bf16[4,3,96,128]{3,2,1,0:T(8,128)(2,1)} %collective-permute-done.17.refs_10_), channel_id=1, source_target_pairs={{0,60},{4,0},{8,4},{12,8},{16,12},{20,16},{24,20},{28,24},{32,28},... | collective-permute-start | bytes 884744 | tf_op jit(solution)/shard_map/ppermute | solution.py:128
  157.8 4.6 %collective-permute-start.34 = (bf16[4,3,96,128]{3,2,1,0:T(8,128)(2,1)}, bf16[4,3,96,128]{3,2,1,0:T(8,128)(2,1)}, u32[]{:S(2)}, u32[]{:S(2)}) collective-permute-start(bf16[4,3,96,128]{3,2,1,0:T(8,128)(2,1)} %collective-permute-done.33.refs_26_), channel_id=1, source_target_pairs={{0,60},{4,0},{8,4},{12,8},{16,12},{20,16},{24,20},{28,24},{32,28},... | collective-permute-start | bytes 884744 | tf_op jit(solution)/shard_map/ppermute | solution.py:128
  167.7 5.5 %collective-permute-done.27.refs_24_ = bf16[4,3,96,128]{3,2,1,0:T(8,128)(2,1)} collective-permute-done((bf16[4,3,96,128]{3,2,1,0:T(8,128)(2,1)}, bf16[4,3,96,128]{3,2,1,0:T(8,128)(2,1)}, u32[]{:S(2)}, u32[]{:S(2)}) %collective-permute-start.27) | collective-permute-done | bytes 294944 | tf_op jit(solution)/shard_map/ppermute | solution.py:126
  173.3 11.3 %experts.1 = bf16[768,2048]{1,0:T(8,128)(2,1)S(1)} custom-call(bf16[4,192,2048]{2,1,0:T(8,128)(2,1)S(1)} %sort_rows.1.rows_ref, bf16[192,192]{1,0:T(8,128)(2,1)S(1)} %copy-done.6, bf16[4,3,96,128]{3,2,1,0:T(8,128)(2,1)} %copy-done.5, bf16[4,3,96,128]{3,2,1,0:T(8,128)(2,1)} %copy-done.14, bf16[4,3,96,128]{3,2,1,0:T(8,128)(2,1)} %copy-done.17, ...), custom_call_target="tpu_custom_call" | custom-call | tf_op jit(solution)/shard_map/experts/pallas_call | solution.py:294
  184.6 61.1 %all_to_all.10 = bf16[32,24,2048]{2,1,0:T(8,128)(2,1)S(1)} all-to-all(bf16[32,24,2048]{2,1,0:T(8,128)(2,1)S(1)} %bitcast.10), channel_id=1, replica_groups=mesh['X'=4,'C'=2,'H'=2,'B'=2,'A'=4,'Y'=4] {'X','C','Y'}, dimensions={0} | all-to-all | bytes 6291456 | tf_op jit(solution)/shard_map/all_to_all | solution.py:358
  (127 shorter events, 49.4 us)
Async XLA Ops:
  6.9 157.7 %all-to-all-start = ((bf16[32,24,2048]{2,1,0:T(8,128)(2,1)}), bf16[32,24,2048]{2,1,0:T(8,128)(2,1)S(1)}, u32[]{:S(2)}, u32[]{:S(2)}) async-start(bf16[32,24,2048]{2,1,0:T(8,128)(2,1)} %bitcast.8), calls=%async_computation | async-start | bytes 6291456 | tf_op jit(solution)/shard_map/all_to_all | solution.py:358
  18.8 15.6 %collective-permute-start = (bf16[2,3,96,128]{3,2,1,0:T(8,128)(2,1)S(1)}, bf16[2,3,96,128]{3,2,1,0:T(8,128)(2,1)S(1)}, u32[]{:S(2)}, u32[]{:S(2)}) collective-permute-start(bf16[2,3,96,128]{3,2,1,0:T(8,128)(2,1)S(1)} %get-tuple-element.8), channel_id=1, source_target_pairs={{0,0},{4,128},{8,256},{12,384},{128,4},{132,132},{136,260},{140,38... | collective-permute-start | bytes 442376 | tf_op jit(solution)/shard_map/ppermute | solution.py:86
  19.5 35.5 %collective-permute-start.1 = (bf16[2,3,96,128]{3,2,1,0:T(8,128)(2,1)S(1)}, bf16[2,3,96,128]{3,2,1,0:T(8,128)(2,1)S(1)}, u32[]{:S(2)}, u32[]{:S(2)}) collective-permute-start(bf16[2,3,96,128]{3,2,1,0:T(8,128)(2,1)S(1)} %get-tuple-element.9), channel_id=1, source_target_pairs={{0,4},{4,132},{8,260},{12,388},{128,8},{132,136},{136,264},{140,39... | collective-permute-start | bytes 442376 | tf_op jit(solution)/shard_map/ppermute | solution.py:86
  25.2 36.4 %collective-permute-start.2 = (bf16[2,3,96,128]{3,2,1,0:T(8,128)(2,1)S(1)}, bf16[2,3,96,128]{3,2,1,0:T(8,128)(2,1)S(1)}, u32[]{:S(2)}, u32[]{:S(2)}) collective-permute-start(bf16[2,3,96,128]{3,2,1,0:T(8,128)(2,1)S(1)} %get-tuple-element.10), channel_id=1, source_target_pairs={{0,8},{4,136},{8,264},{12,392},{128,12},{132,140},{136,268},{140,3... | collective-permute-start | bytes 442376 | tf_op jit(solution)/shard_map/ppermute | solution.py:86
  29.6 32.4 %collective-permute-start.3 = (bf16[2,3,96,128]{3,2,1,0:T(8,128)(2,1)S(1)}, bf16[2,3,96,128]{3,2,1,0:T(8,128)(2,1)S(1)}, u32[]{:S(2)}, u32[]{:S(2)}) collective-permute-start(bf16[2,3,96,128]{3,2,1,0:T(8,128)(2,1)S(1)} %get-tuple-element.11), channel_id=1, source_target_pairs={{0,12},{4,140},{8,268},{12,396},{128,0},{132,128},{136,256},{140,3... | collective-permute-start | bytes 442376 | tf_op jit(solution)/shard_map/ppermute | solution.py:86
  67.6 16.2 %collective-permute-start.20 = (bf16[4,3,96,128]{3,2,1,0:T(8,128)(2,1)S(1)}, bf16[4,3,96,128]{3,2,1,0:T(8,128)(2,1)S(1)}, u32[]{:S(2)}, u32[]{:S(2)}) collective-permute-start(bf16[4,3,96,128]{3,2,1,0:T(8,128)(2,1)S(1)} %collective-permute-done.19.refs_16_), channel_id=1, source_target_pairs={{0,4},{4,8},{8,12},{12,16},{16,20},{20,24},{24,28},{28,32},{32,36}... | collective-permute-start | bytes 884744 | tf_op jit(solution)/shard_map/ppermute | solution.py:126
  69.5 16.2 %collective-permute-start.12 = (bf16[4,3,96,128]{3,2,1,0:T(8,128)(2,1)S(1)}, bf16[4,3,96,128]{3,2,1,0:T(8,128)(2,1)S(1)}, u32[]{:S(2)}, u32[]{:S(2)}) collective-permute-start(bf16[4,3,96,128]{3,2,1,0:T(8,128)(2,1)S(1)} %get-tuple-element.12.refs_0_), channel_id=1, source_target_pairs={{0,60},{4,0},{8,4},{12,8},{16,12},{20,16},{24,20},{28,24},{32,28},... | collective-permute-start | bytes 884744 | tf_op jit(solution)/shard_map/ppermute | solution.py:128
  79.2 13.1 %collective-permute-start.28 = (bf16[4,3,96,128]{3,2,1,0:T(8,128)(2,1)S(1)}, bf16[4,3,96,128]{3,2,1,0:T(8,128)(2,1)S(1)}, u32[]{:S(2)}, u32[]{:S(2)}) collective-permute-start(bf16[4,3,96,128]{3,2,1,0:T(8,128)(2,1)S(1)} %collective-permute-done.19.refs_16_), channel_id=1, source_target_pairs={{0,60},{4,0},{8,4},{12,8},{16,12},{20,16},{24,20},{28,24},{32,28},... | collective-permute-start | bytes 884744 | tf_op jit(solution)/shard_map/ppermute | solution.py:128
  83.8 13.1 %collective-permute-start.21 = (bf16[4,3,96,128]{3,2,1,0:T(8,128)(2,1)S(1)}, bf16[4,3,96,128]{3,2,1,0:T(8,128)(2,1)S(1)}, u32[]{:S(2)}, u32[]{:S(2)}) collective-permute-start(bf16[4,3,96,128]{3,2,1,0:T(8,128)(2,1)S(1)} %collective-permute-done.20.refs_17_), channel_id=1, source_target_pairs={{0,4},{4,8},{8,12},{12,16},{16,20},{20,24},{24,28},{28,32},{32,36}... | collective-permute-start | bytes 884744 | tf_op jit(solution)/shard_map/ppermute | solution.py:126
  85.7 13.1 %collective-permute-start.13 = (bf16[4,3,96,128]{3,2,1,0:T(8,128)(2,1)S(1)}, bf16[4,3,96,128]{3,2,1,0:T(8,128)(2,1)S(1)}, u32[]{:S(2)}, u32[]{:S(2)}) collective-permute-start(bf16[4,3,96,128]{3,2,1,0:T(8,128)(2,1)S(1)} %collective-permute-done.12.refs_15_), channel_id=1, source_target_pairs={{0,60},{4,0},{8,4},{12,8},{16,12},{20,16},{24,20},{28,24},{32,28},... | collective-permute-start | bytes 884744 | tf_op jit(solution)/shard_map/ppermute | solution.py:128
  90.3 13.1 %collective-permute-start.6 = (bf16[4,3,96,128]{3,2,1,0:T(8,128)(2,1)S(1)}, bf16[4,3,96,128]{3,2,1,0:T(8,128)(2,1)S(1)}, u32[]{:S(2)}, u32[]{:S(2)}) collective-permute-start(bf16[4,3,96,128]{3,2,1,0:T(8,128)(2,1)S(1)} %collective-permute-done.5.refs_2_), channel_id=1, source_target_pairs={{0,4},{4,8},{8,12},{12,16},{16,20},{20,24},{24,28},{28,32},{32,36}... | collective-permute-start | bytes 884744 | tf_op jit(solution)/shard_map/ppermute | solution.py:126
  92.3 13.1 %collective-permute-start.29 = (bf16[4,3,96,128]{3,2,1,0:T(8,128)(2,1)S(1)}, bf16[4,3,96,128]{3,2,1,0:T(8,128)(2,1)S(1)}, u32[]{:S(2)}, u32[]{:S(2)}) collective-permute-start(bf16[4,3,96,128]{3,2,1,0:T(8,128)(2,1)S(1)} %collective-permute-done.28.refs_31_), channel_id=1, source_target_pairs={{0,60},{4,0},{8,4},{12,8},{16,12},{20,16},{24,20},{28,24},{32,28},... | collective-permute-start | bytes 884744 | tf_op jit(solution)/shard_map/ppermute | solution.py:128
  96.9 13.1 %collective-permute-start.22 = (bf16[4,3,96,128]{3,2,1,0:T(8,128)(2,1)S(1)}, bf16[4,3,96,128]{3,2,1,0:T(8,128)(2,1)S(1)}, u32[]{:S(2)}, u32[]{:S(2)}) collective-permute-start(bf16[4,3,96,128]{3,2,1,0:T(8,128)(2,1)S(1)} %collective-permute-done.21.refs_18_), channel_id=1, source_target_pairs={{0,4},{4,8},{8,12},{12,16},{16,20},{20,24},{24,28},{28,32},{32,36}... | collective-permute-start | bytes 884744 | tf_op jit(solution)/shard_map/ppermute | solution.py:126
  98.8 13.1 %collective-permute-start.14 = (bf16[4,3,96,128]{3,2,1,0:T(8,128)(2,1)S(1)}, bf16[4,3,96,128]{3,2,1,0:T(8,128)(2,1)S(1)}, u32[]{:S(2)}, u32[]{:S(2)}) collective-permute-start(bf16[4,3,96,128]{3,2,1,0:T(8,128)(2,1)S(1)} %collective-permute-done.13.refs_14_), channel_id=1, source_target_pairs={{0,60},{4,0},{8,4},{12,8},{16,12},{20,16},{24,20},{28,24},{32,28},... | collective-permute-start | bytes 884744 | tf_op jit(solution)/shard_map/ppermute | solution.py:128
  103.4 13.1 %collective-permute-start.7 = (bf16[4,3,96,128]{3,2,1,0:T(8,128)(2,1)S(1)}, bf16[4,3,96,128]{3,2,1,0:T(8,128)(2,1)S(1)}, u32[]{:S(2)}, u32[]{:S(2)}) collective-permute-start(bf16[4,3,96,128]{3,2,1,0:T(8,128)(2,1)S(1)} %collective-permute-done.6.refs_3_), channel_id=1, source_target_pairs={{0,4},{4,8},{8,12},{12,16},{16,20},{20,24},{24,28},{28,32},{32,36}... | collective-permute-start | bytes 884744 | tf_op jit(solution)/shard_map/ppermute | solution.py:126
  105.4 13.1 %collective-permute-start.30 = (bf16[4,3,96,128]{3,2,1,0:T(8,128)(2,1)S(1)}, bf16[4,3,96,128]{3,2,1,0:T(8,128)(2,1)S(1)}, u32[]{:S(2)}, u32[]{:S(2)}) collective-permute-start(bf16[4,3,96,128]{3,2,1,0:T(8,128)(2,1)S(1)} %collective-permute-done.29.refs_30_), channel_id=1, source_target_pairs={{0,60},{4,0},{8,4},{12,8},{16,12},{20,16},{24,20},{28,24},{32,28},... | collective-permute-start | bytes 884744 | tf_op jit(solution)/shard_map/ppermute | solution.py:128
  111.9 13.1 %collective-permute-start.15 = (bf16[4,3,96,128]{3,2,1,0:T(8,128)(2,1)S(1)}, bf16[4,3,96,128]{3,2,1,0:T(8,128)(2,1)S(1)}, u32[]{:S(2)}, u32[]{:S(2)}) collective-permute-start(bf16[4,3,96,128]{3,2,1,0:T(8,128)(2,1)S(1)} %collective-permute-done.14.refs_13_), channel_id=1, source_target_pairs={{0,60},{4,0},{8,4},{12,8},{16,12},{20,16},{24,20},{28,24},{32,28},... | collective-permute-start | bytes 884744 | tf_op jit(solution)/shard_map/ppermute | solution.py:128
  118.5 13.1 %collective-permute-start.31 = (bf16[4,3,96,128]{3,2,1,0:T(8,128)(2,1)S(1)}, bf16[4,3,96,128]{3,2,1,0:T(8,128)(2,1)S(1)}, u32[]{:S(2)}, u32[]{:S(2)}) collective-permute-start(bf16[4,3,96,128]{3,2,1,0:T(8,128)(2,1)S(1)} %collective-permute-done.30.refs_29_), channel_id=1, source_target_pairs={{0,60},{4,0},{8,4},{12,8},{16,12},{20,16},{24,20},{28,24},{32,28},... | collective-permute-start | bytes 884744 | tf_op jit(solution)/shard_map/ppermute | solution.py:128
  125.0 13.1 %collective-permute-start.16 = (bf16[4,3,96,128]{3,2,1,0:T(8,128)(2,1)S(1)}, bf16[4,3,96,128]{3,2,1,0:T(8,128)(2,1)S(1)}, u32[]{:S(2)}, u32[]{:S(2)}) collective-permute-start(bf16[4,3,96,128]{3,2,1,0:T(8,128)(2,1)S(1)} %collective-permute-done.15.refs_12_), channel_id=1, source_target_pairs={{0,60},{4,0},{8,4},{12,8},{16,12},{20,16},{24,20},{28,24},{32,28},... | collective-permute-start | bytes 884744 | tf_op jit(solution)/shard_map/ppermute | solution.py:128
  129.6 13.1 %collective-permute-start.9 = (bf16[4,3,96,128]{3,2,1,0:T(8,128)(2,1)S(1)}, bf16[4,3,96,128]{3,2,1,0:T(8,128)(2,1)S(1)}, u32[]{:S(2)}, u32[]{:S(2)}) collective-permute-start(bf16[4,3,96,128]{3,2,1,0:T(8,128)(2,1)S(1)} %collective-permute-done.8.refs_5_), channel_id=1, source_target_pairs={{0,4},{4,8},{8,12},{12,16},{16,20},{20,24},{24,28},{28,32},{32,36}... | collective-permute-start | bytes 884744 | tf_op jit(solution)/shard_map/ppermute | solution.py:126
  131.6 13.1 %collective-permute-start.32 = (bf16[4,3,96,128]{3,2,1,0:T(8,128)(2,1)S(1)}, bf16[4,3,96,128]{3,2,1,0:T(8,128)(2,1)S(1)}, u32[]{:S(2)}, u32[]{:S(2)}) collective-permute-start(bf16[4,3,96,128]{3,2,1,0:T(8,128)(2,1)S(1)} %collective-permute-done.31.refs_28_), channel_id=1, source_target_pairs={{0,60},{4,0},{8,4},{12,8},{16,12},{20,16},{24,20},{28,24},{32,28},... | collective-permute-start | bytes 884744 | tf_op jit(solution)/shard_map/ppermute | solution.py:128
  136.2 13.1 %collective-permute-start.25 = (bf16[4,3,96,128]{3,2,1,0:T(8,128)(2,1)S(1)}, bf16[4,3,96,128]{3,2,1,0:T(8,128)(2,1)S(1)}, u32[]{:S(2)}, u32[]{:S(2)}) collective-permute-start(bf16[4,3,96,128]{3,2,1,0:T(8,128)(2,1)S(1)} %collective-permute-done.24.refs_21_), channel_id=1, source_target_pairs={{0,4},{4,8},{8,12},{12,16},{16,20},{20,24},{24,28},{28,32},{32,36}... | collective-permute-start | bytes 884744 | tf_op jit(solution)/shard_map/ppermute | solution.py:126
  138.1 13.1 %collective-permute-start.17 = (bf16[4,3,96,128]{3,2,1,0:T(8,128)(2,1)S(1)}, bf16[4,3,96,128]{3,2,1,0:T(8,128)(2,1)}, u32[]{:S(2)}, u32[]{:S(2)}) collective-permute-start(bf16[4,3,96,128]{3,2,1,0:T(8,128)(2,1)S(1)} %collective-permute-done.16.refs_11_), channel_id=1, source_target_pairs={{0,60},{4,0},{8,4},{12,8},{16,12},{20,16},{24,20},{28,24},{32,28},... | collective-permute-start | bytes 884744 | tf_op jit(solution)/shard_map/ppermute | solution.py:128
  151.2 14.5 %collective-permute-start.18 = (bf16[4,3,96,128]{3,2,1,0:T(8,128)(2,1)}, bf16[4,3,96,128]{3,2,1,0:T(8,128)(2,1)}, u32[]{:S(2)}, u32[]{:S(2)}) collective-permute-start(bf16[4,3,96,128]{3,2,1,0:T(8,128)(2,1)} %collective-permute-done.17.refs_10_), channel_id=1, source_target_pairs={{0,60},{4,0},{8,4},{12,8},{16,12},{20,16},{24,20},{28,24},{32,28},... | collective-permute-start | bytes 884744 | tf_op jit(solution)/shard_map/ppermute | solution.py:128
  (48 other events, 1878.3 us)
where the time goes:
time: 250 us; the launch traced here: 249 us
  starting transfers between devices  124 us (50%)
  blocking collectives  61.1 us (24%)
  waiting for transfers between devices  38.4 us (15%)
  Pallas kernels  18.6 us (7%)
  local copies, waits for them, and re-layouts  5.23 us (2%)
    ppermute x14, starting transfers between devices, around(): found[i][Z - k] = lax.ppermute(found[i][(Z - k + 1) % Z], axes, DOWN)  64 us
    all_to_all x1, blocking collectives, exchange(): lax.all_to_all(blocks, ('X', 'C', 'Y'), 0, 0, tiled=True).reshape(ROWS, D)  61.1 us
    ppermute x16, starting transfers between devices, around(): found[i][k] = lax.ppermute(found[i][k - 1], axes, UP)  30.9 us
    ppermute x4, waiting for transfers between devices, send_home(): moved.append(lax.ppermute(pieces[r], ('X', 'A'), pairs))  27.6 us
    ppermute x4, starting transfers between devices, send_home(): moved.append(lax.ppermute(pieces[r], ('X', 'A'), pairs))  15.5 us
    pallas_call x1, Pallas kernels, experts(): pl.pallas_call(expert_kernel, out_shape=pltpu.VMEM((ROWS, D), BF), in_spe...  11.3 us
    all_to_all x1, starting transfers between devices, exchange(): lax.all_to_all(blocks, ('X', 'C', 'Y'), 0, 0, tiled=True).reshape(ROWS, D)  10.7 us
    ppermute x16, waiting for transfers between devices, around(): found[i][k] = lax.ppermute(found[i][k - 1], axes, UP)  10.1 us
  transfers between devices with their start and end apart: 36, of which 7 were waited for; matrix products, arithmetic and copies ran while one was open for 0% of the time, Pallas kernels for 1%

commit v1 on v0

--- a/solution.py
+++ b/solution.py
@@ -88,13 +88,11 @@
 
 
 def place_kernel(*refs):
-    keep_ref, give_ref, sem = refs[X:]
-    a, c = lax.axis_index("A"), lax.axis_index("C")
-    copies = []
-    for r in range(X):
-        at = (a - r) & 3
-        copies.append(pltpu.make_async_copy(refs[r].at[c], keep_ref.at[at], sem))
-        copies.append(pltpu.make_async_copy(refs[r].at[1 - c], give_ref.at[at], sem))
+    out_ref, sem = refs[X:]
+    a = lax.axis_index("A")
+    copies = [
+        pltpu.make_async_copy(refs[r], out_ref.at[:, (a - r) & 3], sem) for r in range(X)
+    ]
     for copy in copies:
         copy.start()
     for copy in copies:
@@ -104,9 +102,9 @@
 def place(pieces):
     return pl.pallas_call(
         place_kernel,
-        out_shape=(pltpu.VMEM((X, 3, 96, 128), BF),) * 2,
+        out_shape=pltpu.VMEM((2, X, 3, 96, 128), BF),
         in_specs=[pl.BlockSpec(memory_space=pl.ANY)] * X,
-        out_specs=tuple(whole(2)),
+        out_specs=pl.BlockSpec(memory_space=VMEM),
         scratch_shapes=[pltpu.SemaphoreType.DMA],
         compiler_params=params(),
         name="place",
@@ -118,15 +116,15 @@
 DOWN = [(z, (z - 1) % Z) for z in range(Z)]
 
 
-def around(halves):
-    found = [[half] + [None] * (Z - 1) for half in halves]
-    axes = ("H", "B", "A")
-    for k in range(1, Z // 2 + 1):
-        for i in range(2):
-            found[i][k] = lax.ppermute(found[i][k - 1], axes, UP)
-            if k < Z // 2:
-                found[i][Z - k] = lax.ppermute(found[i][(Z - k + 1) % Z], axes, DOWN)
-    return [pltpu.with_memory_space_constraint(f, pltpu.HBM) for f in found[0] + found[1]]
+def around(piece):
+    axes, half = ("H", "B", "A"), Z // 2
+    found = [piece] + [None] * (Z - 1)
+    for k in range(1, half):
+        found[k] = lax.ppermute(found[k - 1], axes, UP)
+        found[Z - k] = lax.ppermute(found[(Z - k + 1) % Z], axes, DOWN)
+    found[half] = lax.ppermute(found[half - 1][0], axes, UP)
+    found.append(lax.ppermute(found[half + 1][1], axes, DOWN))
+    return [pltpu.with_memory_space_constraint(f, pltpu.HBM) for f in found]
 
 
 def route_rows(ids0, ids1):
@@ -215,26 +213,34 @@
 
 
 def expert_kernel(rows_ref, to_natural_ref, *refs):
-    pieces, (out_ref, in_mats, down_mat, sem) = refs[: 2 * Z], refs[2 * Z :]
+    pieces, (out_ref, in_mats, down_mat, sem) = refs[: Z + 1], refs[Z + 1 :]
     me = (lax.axis_index("H") * B + lax.axis_index("B")) * A + lax.axis_index("A")
-    core = lax.axis_index("C")
     copies = []
-    for i in range(2):
-        c = core if i == 0 else 1 - core
-        for k in range(Z):
-            z = (me - k) & (Z - 1)
-            h, b, q = z >> 3, (z >> 2) & 1, z & 3
-            ref = pieces[i * Z + k]
+    for k in range(Z):
+        z = (me - k) & (Z - 1)
+        h, b, q = z >> 3, (z >> 2) & 1, z & 3
+        if k == Z // 2:
+            parts = [((c,), (), pieces[k if c == 0 else Z]) for c in range(2)]
+        else:
+            every = slice(None)
+            parts = [((every,), (every,), pieces[k])]
+        for to, lead, ref in parts:
             for m in range(2):
                 for f in range(3):
                     copies.append(
                         pltpu.make_async_copy(
-                            ref.at[:, m, pl.ds(f * 32, 32), :],
-                            in_mats.at[b, m, c, :, h, q, :, pl.ds(f * 128, 128)],
+                            ref.at[(*lead, slice(None), m, pl.ds(f * 32, 32))],
+                            in_mats.at[
+                                (b, m, *to, slice(None), h, q, slice(None), pl.ds(f * 128, 128))
+                            ],
                             sem,
                         )
                     )
-            copies.append(pltpu.make_async_copy(ref.at[:, 2], down_mat.at[b, c, :, h, q], sem))
+            copies.append(
+                pltpu.make_async_copy(
+                    ref.at[(*lead, slice(None), 2)], down_mat.at[(b, *to, slice(None), h, q)], sem
+                )
+            )
     for copy in copies:
         copy.start()
     for copy in copies:
@@ -294,7 +300,7 @@
     return pl.pallas_call(
         expert_kernel,
         out_shape=pltpu.VMEM((ROWS, D), BF),
-        in_specs=whole(2) + [pl.BlockSpec(memory_space=pl.ANY)] * (2 * Z),
+        in_specs=whole(2) + [pl.BlockSpec(memory_space=pl.ANY)] * (Z + 1),
         out_specs=pl.BlockSpec(memory_space=VMEM),
         scratch_shapes=[
             VMEM((B, 2, C, X, H, A, 32, FW), BF),
@@ -362,8 +368,8 @@
     gain = norm_gain.reshape(1, D)
     ids, codes = expert_ids.T, gate_codes.T
     to_natural = sort_matrix()
-    keep, give = place(send_home(split_weights(w_gate, w_up, w_down)))
-    weights = around((keep, lax.ppermute(give, "C", [(0, 1), (1, 0)])))
+    pieces = place(send_home(split_weights(w_gate, w_up, w_down)))
+    weights = around(lax.all_to_all(pieces, "C", 0, 0, tiled=True))
     sent = dispatch(ids, hidden_in, gain, out_grad)
     arrived = exchange(sent)
     rows = sort_rows(jnp.asarray(to_natural.T, BF), arrived)

time: 250 us -> 248 us (level)
  waiting for transfers between devices: 38.4 us -> 80.3 us
  starting transfers between devices: 124 us -> 89.5 us
  blocking collectives: 61.1 us -> 54.1 us
    ppermute x31 -> x16, waiting for transfers between devices: 10.8 us -> 72.2 us  [the longest x7 37.1 us: around(): found[Z - k] = lax.ppermute(found[(Z - k + 1) % Z], axes, DOWN)]
    ppermute x31 -> x16, starting transfers between devices: 97.8 us -> 58.6 us  [the longest x7 38 us: around(): found[Z - k] = lax.ppermute(found[(Z - k + 1) % Z], axes, DOWN)]
    ppermute x4, waiting for transfers between devices: 27.6 us -> 8.1 us  [send_home(): moved.append(lax.ppermute(pieces[r], ('X', 'A'), pairs))]
    all_to_all x1, blocking collectives: 61.1 us -> 49.7 us  [exchange(): lax.all_to_all(blocks, ('X', 'C', 'Y'), 0, 0, tiled=True).reshape(ROWS, D)]
    all_to_all x0 -> x1, blocking collectives: none -> 4.33 us  [body(): weights = around(lax.all_to_all(pieces, 'C', 0, 0, tiled=True))]
    ppermute x4, starting transfers between devices: 15.5 us -> 18.2 us  [send_home(): moved.append(lax.ppermute(pieces[r], ('X', 'A'), pairs))]
    unnamed x72 -> x46, local copies, waits for them, and re-layouts: 5.23 us -> 3.24 us
  transfers between devices with their start and end apart: 36 -> 21, of which waited for: 7 -> 9; matrix products, arithmetic and copies ran while one was open for 0% -> 0% of each run, Pallas kernels for 1% -> 1%
where the time goes in v1:
time: 248 us; the launch traced here: 247 us
  starting transfers between devices  89.5 us (36%)
  waiting for transfers between devices  80.3 us (32%)
  blocking collectives  54.1 us (22%)
  Pallas kernels  18.1 us (7%)
  local copies, waits for them, and re-layouts  4.06 us (2%)
    all_to_all x1, blocking collectives, exchange(): lax.all_to_all(blocks, ('X', 'C', 'Y'), 0, 0, tiled=True).reshape(ROWS, D)  49.7 us
    ppermute x7, starting transfers between devices, around(): found[Z - k] = lax.ppermute(found[(Z - k + 1) % Z], axes, DOWN)  38 us
    ppermute x7, waiting for transfers between devices, around(): found[Z - k] = lax.ppermute(found[(Z - k + 1) % Z], axes, DOWN)  37.1 us
    ppermute x7, waiting for transfers between devices, around(): found[k] = lax.ppermute(found[k - 1], axes, UP)  32.2 us
    ppermute x4, starting transfers between devices, send_home(): moved.append(lax.ppermute(pieces[r], ('X', 'A'), pairs))  18.2 us
    ppermute x7, starting transfers between devices, around(): found[k] = lax.ppermute(found[k - 1], axes, UP)  13.4 us
    all_to_all x1, starting transfers between devices, exchange(): lax.all_to_all(blocks, ('X', 'C', 'Y'), 0, 0, tiled=True).reshape(ROWS, D)  12.7 us
    pallas_call x1, Pallas kernels, experts(): pl.pallas_call(expert_kernel, out_shape=pltpu.VMEM((ROWS, D), BF), in_spe...  11.2 us
  transfers between devices with their start and end apart: 21, of which 9 were waited for; matrix products, arithmetic and copies ran while one was open for 0% of the time, Pallas kernels for 1%

profile of v1, /device:TPU:1, one launch (start us, length us, event | category | flops | bytes accessed | tf_op | source)
XLA Modules:
  0.0 247.3 jit_solution(7724213256292058880)
XLA Ops:
  2.5 6.4 %collective-permute-start.1 = (bf16[2,3,96,128]{3,2,1,0:T(8,128)(2,1)S(1)}, bf16[2,3,96,128]{3,2,1,0:T(8,128)(2,1)S(1)}, u32[]{:S(2)}, u32[]{:S(2)}) collective-permute-start(bf16[2,3,96,128]{3,2,1,0:T(8,128)(2,1)S(1)} %get-tuple-element.7), channel_id=1, source_target_pairs={{0,4},{4,132},{8,260},{12,388},{128,8},{132,136},{136,264},{140,39... | collective-permute-start | bytes 442376 | tf_op jit(solution)/shard_map/ppermute | solution.py:86
  8.9 6.4 %collective-permute-start.2 = (bf16[2,3,96,128]{3,2,1,0:T(8,128)(2,1)S(1)}, bf16[2,3,96,128]{3,2,1,0:T(8,128)(2,1)S(1)}, u32[]{:S(2)}, u32[]{:S(2)}) collective-permute-start(bf16[2,3,96,128]{3,2,1,0:T(8,128)(2,1)S(1)} %get-tuple-element.8), channel_id=1, source_target_pairs={{0,8},{4,136},{8,264},{12,392},{128,12},{132,140},{136,268},{140,3... | collective-permute-start | bytes 442376 | tf_op jit(solution)/shard_map/ppermute | solution.py:86
  15.3 4.8 %collective-permute-start.3 = (bf16[2,3,96,128]{3,2,1,0:T(8,128)(2,1)S(1)}, bf16[2,3,96,128]{3,2,1,0:T(8,128)(2,1)S(1)}, u32[]{:S(2)}, u32[]{:S(2)}) collective-permute-start(bf16[2,3,96,128]{3,2,1,0:T(8,128)(2,1)S(1)} %get-tuple-element.9), channel_id=1, source_target_pairs={{0,12},{4,140},{8,268},{12,396},{128,0},{132,128},{136,256},{140,3... | collective-permute-start | bytes 442376 | tf_op jit(solution)/shard_map/ppermute | solution.py:86
  20.1 8.1 %collective-permute-done.3.refs_3_ = bf16[2,3,96,128]{3,2,1,0:T(8,128)(2,1)S(1)} collective-permute-done((bf16[2,3,96,128]{3,2,1,0:T(8,128)(2,1)S(1)}, bf16[2,3,96,128]{3,2,1,0:T(8,128)(2,1)S(1)}, u32[]{:S(2)}, u32[]{:S(2)}) %collective-permute-start.3) | collective-permute-done | bytes 147488 | tf_op jit(solution)/shard_map/ppermute | solution.py:86
  28.6 4.3 %all_to_all.15.refs_0_ = bf16[2,4,3,96,128]{4,3,2,1,0:T(8,128)(2,1)S(1)} all-to-all(bf16[2,4,3,96,128]{4,3,2,1,0:T(8,128)(2,1)S(1)} %place.1), channel_id=1, replica_groups=mesh['X'=4,'C'=2,'H'=2,'B'=2,'A'=4,'Y'=4] {'C'}, dimensions={0} | all-to-all | bytes 1179648 | tf_op jit(solution)/shard_map/all_to_all | solution.py:372
  34.8 6.7 %collective-permute-start.12 = (bf16[2,4,3,96,128]{4,3,2,1,0:T(8,128)(2,1)S(1)}, bf16[2,4,3,96,128]{4,3,2,1,0:T(8,128)(2,1)S(1)}, u32[]{:S(2)}, u32[]{:S(2)}) collective-permute-start(bf16[2,4,3,96,128]{4,3,2,1,0:T(8,128)(2,1)S(1)} %all_to_all.15.refs_0_), channel_id=1, source_target_pairs={{0,60},{4,0},{8,4},{12,8},{16,12},{20,16},{24,20},{28,24},{32,28},... | collective-permute-start | bytes 1769480 | tf_op jit(solution)/shard_map/ppermute | solution.py:124
  41.5 11.4 %collective-permute-done.4.refs_1_ = bf16[2,4,3,96,128]{4,3,2,1,0:T(8,128)(2,1)S(1)} collective-permute-done((bf16[2,4,3,96,128]{4,3,2,1,0:T(8,128)(2,1)S(1)}, bf16[2,4,3,96,128]{4,3,2,1,0:T(8,128)(2,1)S(1)}, u32[]{:S(2)}, u32[]{:S(2)}) %collective-permute-start.4) | collective-permute-done | bytes 589856 | tf_op jit(solution)/shard_map/ppermute | solution.py:123
  54.8 6.1 %collective-permute-start.13 = (bf16[2,4,3,96,128]{4,3,2,1,0:T(8,128)(2,1)S(1)}, bf16[2,4,3,96,128]{4,3,2,1,0:T(8,128)(2,1)}, u32[]{:S(2)}, u32[]{:S(2)}) collective-permute-start(bf16[2,4,3,96,128]{4,3,2,1,0:T(8,128)(2,1)S(1)} %collective-permute-done.12.refs_15_), channel_id=1, source_target_pairs={{0,60},{4,0},{8,4},{12,8},{16,12},{20,16},{24,20},{28,24},{32,28},... | collective-permute-start | bytes 1769480 | tf_op jit(solution)/shard_map/ppermute | solution.py:124
  60.9 10.8 %collective-permute-done.5.refs_2_ = bf16[2,4,3,96,128]{4,3,2,1,0:T(8,128)(2,1)S(1)} collective-permute-done((bf16[2,4,3,96,128]{4,3,2,1,0:T(8,128)(2,1)S(1)}, bf16[2,4,3,96,128]{4,3,2,1,0:T(8,128)(2,1)S(1)}, u32[]{:S(2)}, u32[]{:S(2)}) %collective-permute-start.5) | collective-permute-done | bytes 589856 | tf_op jit(solution)/shard_map/ppermute | solution.py:123
  73.6 4.6 %collective-permute-start.14 = (bf16[2,4,3,96,128]{4,3,2,1,0:T(8,128)(2,1)}, bf16[2,4,3,96,128]{4,3,2,1,0:T(8,128)(2,1)}, u32[]{:S(2)}, u32[]{:S(2)}) collective-permute-start(bf16[2,4,3,96,128]{4,3,2,1,0:T(8,128)(2,1)} %collective-permute-done.13.refs_14_), channel_id=1, source_target_pairs={{0,60},{4,0},{8,4},{12,8},{16,12},{20,16},{24,20},{28,24},{32,28},... | collective-permute-start | bytes 1769480 | tf_op jit(solution)/shard_map/ppermute | solution.py:124
  78.2 10.1 %collective-permute-done.6.refs_3_ = bf16[2,4,3,96,128]{4,3,2,1,0:T(8,128)(2,1)} collective-permute-done((bf16[2,4,3,96,128]{4,3,2,1,0:T(8,128)(2,1)S(1)}, bf16[2,4,3,96,128]{4,3,2,1,0:T(8,128)(2,1)}, u32[]{:S(2)}, u32[]{:S(2)}) %collective-permute-start.6) | collective-permute-done | bytes 589856 | tf_op jit(solution)/shard_map/ppermute | solution.py:123
  94.5 12.7 %all-to-all-start = ((bf16[32,24,2048]{2,1,0:T(8,128)(2,1)}), bf16[32,24,2048]{2,1,0:T(8,128)(2,1)S(1)}, u32[]{:S(2)}, u32[]{:S(2)}) async-start(bf16[32,24,2048]{2,1,0:T(8,128)(2,1)} %bitcast.12), calls=%async_computation | async-start | bytes 6291456 | tf_op jit(solution)/shard_map/all_to_all | solution.py:364
  107.2 4.9 %collective-permute-start.15 = (bf16[2,4,3,96,128]{4,3,2,1,0:T(8,128)(2,1)}, bf16[2,4,3,96,128]{4,3,2,1,0:T(8,128)(2,1)S(1)}, u32[]{:S(2)}, u32[]{:S(2)}) collective-permute-start(bf16[2,4,3,96,128]{4,3,2,1,0:T(8,128)(2,1)} %collective-permute-done.14.refs_13_), channel_id=1, source_target_pairs={{0,60},{4,0},{8,4},{12,8},{16,12},{20,16},{24,20},{28,24},{32,28},... | collective-permute-start | bytes 1769480 | tf_op jit(solution)/shard_map/ppermute | solution.py:124
  114.0 10.8 %collective-permute-done.15.refs_12_ = bf16[2,4,3,96,128]{4,3,2,1,0:T(8,128)(2,1)S(1)} collective-permute-done((bf16[2,4,3,96,128]{4,3,2,1,0:T(8,128)(2,1)}, bf16[2,4,3,96,128]{4,3,2,1,0:T(8,128)(2,1)S(1)}, u32[]{:S(2)}, u32[]{:S(2)}) %collective-permute-start.15) | collective-permute-done | bytes 589856 | tf_op jit(solution)/shard_map/ppermute | solution.py:124
  124.8 5.2 %collective-permute-start.16 = (bf16[2,4,3,96,128]{4,3,2,1,0:T(8,128)(2,1)S(1)}, bf16[2,4,3,96,128]{4,3,2,1,0:T(8,128)(2,1)S(1)}, u32[]{:S(2)}, u32[]{:S(2)}) collective-permute-start(bf16[2,4,3,96,128]{4,3,2,1,0:T(8,128)(2,1)S(1)} %collective-permute-done.15.refs_12_), channel_id=1, source_target_pairs={{0,60},{4,0},{8,4},{12,8},{16,12},{20,16},{24,20},{28,24},{32,28},... | collective-permute-start | bytes 1769480 | tf_op jit(solution)/shard_map/ppermute | solution.py:124
  132.0 9.6 %collective-permute-done.16.refs_11_ = bf16[2,4,3,96,128]{4,3,2,1,0:T(8,128)(2,1)S(1)} collective-permute-done((bf16[2,4,3,96,128]{4,3,2,1,0:T(8,128)(2,1)S(1)}, bf16[2,4,3,96,128]{4,3,2,1,0:T(8,128)(2,1)S(1)}, u32[]{:S(2)}, u32[]{:S(2)}) %collective-permute-start.16) | collective-permute-done | bytes 589856 | tf_op jit(solution)/shard_map/ppermute | solution.py:124
  141.6 5.3 %collective-permute-start.17 = (bf16[2,4,3,96,128]{4,3,2,1,0:T(8,128)(2,1)S(1)}, bf16[2,4,3,96,128]{4,3,2,1,0:T(8,128)(2,1)S(1)}, u32[]{:S(2)}, u32[]{:S(2)}) collective-permute-start(bf16[2,4,3,96,128]{4,3,2,1,0:T(8,128)(2,1)S(1)} %collective-permute-done.16.refs_11_), channel_id=1, source_target_pairs={{0,60},{4,0},{8,4},{12,8},{16,12},{20,16},{24,20},{28,24},{32,28},... | collective-permute-start | bytes 1769480 | tf_op jit(solution)/shard_map/ppermute | solution.py:124
  148.8 8.8 %collective-permute-done.17.refs_10_ = bf16[2,4,3,96,128]{4,3,2,1,0:T(8,128)(2,1)S(1)} collective-permute-done((bf16[2,4,3,96,128]{4,3,2,1,0:T(8,128)(2,1)S(1)}, bf16[2,4,3,96,128]{4,3,2,1,0:T(8,128)(2,1)S(1)}, u32[]{:S(2)}, u32[]{:S(2)}) %collective-permute-start.17) | collective-permute-done | bytes 589856 | tf_op jit(solution)/shard_map/ppermute | solution.py:124
  157.6 5.3 %collective-permute-start.18 = (bf16[2,4,3,96,128]{4,3,2,1,0:T(8,128)(2,1)S(1)}, bf16[2,4,3,96,128]{4,3,2,1,0:T(8,128)(2,1)S(1)}, u32[]{:S(2)}, u32[]{:S(2)}) collective-permute-start(bf16[2,4,3,96,128]{4,3,2,1,0:T(8,128)(2,1)S(1)} %collective-permute-done.17.refs_10_), channel_id=1, source_target_pairs={{0,60},{4,0},{8,4},{12,8},{16,12},{20,16},{24,20},{28,24},{32,28},... | collective-permute-start | bytes 1769480 | tf_op jit(solution)/shard_map/ppermute | solution.py:124
  164.9 7.9 %collective-permute-done.18.refs_9_ = bf16[2,4,3,96,128]{4,3,2,1,0:T(8,128)(2,1)S(1)} collective-permute-done((bf16[2,4,3,96,128]{4,3,2,1,0:T(8,128)(2,1)S(1)}, bf16[2,4,3,96,128]{4,3,2,1,0:T(8,128)(2,1)S(1)}, u32[]{:S(2)}, u32[]{:S(2)}) %collective-permute-start.18) | collective-permute-done | bytes 589856 | tf_op jit(solution)/shard_map/ppermute | solution.py:124
  173.7 5.3 %collective-permute-start.19 = (bf16[4,3,96,128]{3,2,1,0:T(8,128)(2,1)}, bf16[4,3,96,128]{3,2,1,0:T(8,128)(2,1)}, u32[]{:S(2)}, u32[]{:S(2)}) collective-permute-start(bf16[4,3,96,128]{3,2,1,0:T(8,128)(2,1)} %slice_bitcast_fusion), channel_id=1, source_target_pairs={{0,60},{4,0},{8,4},{12,8},{16,12},{20,16},{24,20},{28,24},{32,28},... | collective-permute-start | bytes 884744 | tf_op jit(solution)/shard_map/ppermute | solution.py:126
  183.0 11.2 %experts.1 = bf16[768,2048]{1,0:T(8,128)(2,1)S(1)} custom-call(bf16[4,192,2048]{2,1,0:T(8,128)(2,1)S(1)} %sort_rows.1.rows_ref, bf16[192,192]{1,0:T(8,128)(2,1)S(1)} %copy-done.5, bf16[2,4,3,96,128]{4,3,2,1,0:T(8,128)(2,1)} %copy-done.12, bf16[2,4,3,96,128]{4,3,2,1,0:T(8,128)(2,1)} %copy-done.15, bf16[2,4,3,96,128]{4,3,2,1,0:T(8,128)(2,1)} %copy-done.17, ...), custom_call_target="tpu_custom_call" | custom-call | tf_op jit(solution)/shard_map/experts/pallas_call | solution.py:300
  194.3 49.7 %all_to_all.16 = bf16[32,24,2048]{2,1,0:T(8,128)(2,1)S(1)} all-to-all(bf16[32,24,2048]{2,1,0:T(8,128)(2,1)S(1)} %bitcast.14), channel_id=1, replica_groups=mesh['X'=4,'C'=2,'H'=2,'B'=2,'A'=4,'Y'=4] {'X','C','Y'}, dimensions={0} | all-to-all | bytes 6291456 | tf_op jit(solution)/shard_map/all_to_all | solution.py:364
  244.1 3.2 %combine.1 = (bf16[128,2048]{1,0:T(8,128)(2,1)}, bf16[128,2048]{1,0:T(8,128)(2,1)}) custom-call(s32[2,128]{1,0:T(2,128)S(1)} %bitcast.18, s32[2,128]{1,0:T(2,128)S(1)} %bitcast.19, bf16[768,2048]{1,0:T(8,128)(2,1)S(1)} %bitcast.13, bf16[128,2048]{1,0:T(8,128)(2,1)S(1)} %copy-done.2, f32[1,2048]{1,0:T(1,128)S(1)} %bitcast.16, bf16[128,2048]{1,0:T(8,128)(2,1)S(1)} %copy-done.4), custom_call_target="tpu_custom_call" | custom-call | tf_op jit(solution)/shard_map/combine/pallas_call | solution.py:352
  (74 shorter events, 26.7 us)
Async XLA Ops:
  0.6 89.6 %copy-start.1 = (bf16[128,2048]{1,0:T(8,128)(2,1)S(1)}, bf16[128,2048]{1,0:T(8,128)(2,1)}, u32[]{:S(2)}) copy-start(bf16[128,2048]{1,0:T(8,128)(2,1)} %hidden_ref.3) | copy-start | bytes 1572868
  0.6 89.6 %copy-start.3 = (bf16[128,2048]{1,0:T(8,128)(2,1)S(1)}, bf16[128,2048]{1,0:T(8,128)(2,1)}, u32[]{:S(2)}) copy-start(bf16[128,2048]{1,0:T(8,128)(2,1)} %grad_ref.3) | copy-start | bytes 1572868
  1.8 18.2 %collective-permute-start = (bf16[2,3,96,128]{3,2,1,0:T(8,128)(2,1)S(1)}, bf16[2,3,96,128]{3,2,1,0:T(8,128)(2,1)S(1)}, u32[]{:S(2)}, u32[]{:S(2)}) collective-permute-start(bf16[2,3,96,128]{3,2,1,0:T(8,128)(2,1)S(1)} %get-tuple-element.6), channel_id=1, source_target_pairs={{0,0},{4,128},{8,256},{12,384},{128,4},{132,132},{136,260},{140,38... | collective-permute-start | bytes 442376 | tf_op jit(solution)/shard_map/ppermute | solution.py:86
  2.5 17.6 %collective-permute-start.1 = (bf16[2,3,96,128]{3,2,1,0:T(8,128)(2,1)S(1)}, bf16[2,3,96,128]{3,2,1,0:T(8,128)(2,1)S(1)}, u32[]{:S(2)}, u32[]{:S(2)}) collective-permute-start(bf16[2,3,96,128]{3,2,1,0:T(8,128)(2,1)S(1)} %get-tuple-element.7), channel_id=1, source_target_pairs={{0,4},{4,132},{8,260},{12,388},{128,8},{132,136},{136,264},{140,39... | collective-permute-start | bytes 442376 | tf_op jit(solution)/shard_map/ppermute | solution.py:86
  8.9 11.2 %collective-permute-start.2 = (bf16[2,3,96,128]{3,2,1,0:T(8,128)(2,1)S(1)}, bf16[2,3,96,128]{3,2,1,0:T(8,128)(2,1)S(1)}, u32[]{:S(2)}, u32[]{:S(2)}) collective-permute-start(bf16[2,3,96,128]{3,2,1,0:T(8,128)(2,1)S(1)} %get-tuple-element.8), channel_id=1, source_target_pairs={{0,8},{4,136},{8,264},{12,392},{128,12},{132,140},{136,268},{140,3... | collective-permute-start | bytes 442376 | tf_op jit(solution)/shard_map/ppermute | solution.py:86
  15.3 12.9 %collective-permute-start.3 = (bf16[2,3,96,128]{3,2,1,0:T(8,128)(2,1)S(1)}, bf16[2,3,96,128]{3,2,1,0:T(8,128)(2,1)S(1)}, u32[]{:S(2)}, u32[]{:S(2)}) collective-permute-start(bf16[2,3,96,128]{3,2,1,0:T(8,128)(2,1)S(1)} %get-tuple-element.9), channel_id=1, source_target_pairs={{0,12},{4,140},{8,268},{12,396},{128,0},{132,128},{136,256},{140,3... | collective-permute-start | bytes 442376 | tf_op jit(solution)/shard_map/ppermute | solution.py:86
  32.9 20.0 %collective-permute-start.4 = (bf16[2,4,3,96,128]{4,3,2,1,0:T(8,128)(2,1)S(1)}, bf16[2,4,3,96,128]{4,3,2,1,0:T(8,128)(2,1)S(1)}, u32[]{:S(2)}, u32[]{:S(2)}) collective-permute-start(bf16[2,4,3,96,128]{4,3,2,1,0:T(8,128)(2,1)S(1)} %all_to_all.15.refs_0_), channel_id=1, source_target_pairs={{0,4},{4,8},{8,12},{12,16},{16,20},{20,24},{24,28},{28,32},{32,36}... | collective-permute-start | bytes 1769480 | tf_op jit(solution)/shard_map/ppermute | solution.py:123
  34.8 20.0 %collective-permute-start.12 = (bf16[2,4,3,96,128]{4,3,2,1,0:T(8,128)(2,1)S(1)}, bf16[2,4,3,96,128]{4,3,2,1,0:T(8,128)(2,1)S(1)}, u32[]{:S(2)}, u32[]{:S(2)}) collective-permute-start(bf16[2,4,3,96,128]{4,3,2,1,0:T(8,128)(2,1)S(1)} %all_to_all.15.refs_0_), channel_id=1, source_target_pairs={{0,60},{4,0},{8,4},{12,8},{16,12},{20,16},{24,20},{28,24},{32,28},... | collective-permute-start | bytes 1769480 | tf_op jit(solution)/shard_map/ppermute | solution.py:124
  52.9 18.8 %collective-permute-start.5 = (bf16[2,4,3,96,128]{4,3,2,1,0:T(8,128)(2,1)S(1)}, bf16[2,4,3,96,128]{4,3,2,1,0:T(8,128)(2,1)S(1)}, u32[]{:S(2)}, u32[]{:S(2)}) collective-permute-start(bf16[2,4,3,96,128]{4,3,2,1,0:T(8,128)(2,1)S(1)} %collective-permute-done.4.refs_1_), channel_id=1, source_target_pairs={{0,4},{4,8},{8,12},{12,16},{16,20},{20,24},{24,28},{28,32},{32,36}... | collective-permute-start | bytes 1769480 | tf_op jit(solution)/shard_map/ppermute | solution.py:123
  54.8 18.8 %collective-permute-start.13 = (bf16[2,4,3,96,128]{4,3,2,1,0:T(8,128)(2,1)S(1)}, bf16[2,4,3,96,128]{4,3,2,1,0:T(8,128)(2,1)}, u32[]{:S(2)}, u32[]{:S(2)}) collective-permute-start(bf16[2,4,3,96,128]{4,3,2,1,0:T(8,128)(2,1)S(1)} %collective-permute-done.12.refs_15_), channel_id=1, source_target_pairs={{0,60},{4,0},{8,4},{12,8},{16,12},{20,16},{24,20},{28,24},{32,28},... | collective-permute-start | bytes 1769480 | tf_op jit(solution)/shard_map/ppermute | solution.py:124
  71.7 16.6 %collective-permute-start.6 = (bf16[2,4,3,96,128]{4,3,2,1,0:T(8,128)(2,1)S(1)}, bf16[2,4,3,96,128]{4,3,2,1,0:T(8,128)(2,1)}, u32[]{:S(2)}, u32[]{:S(2)}) collective-permute-start(bf16[2,4,3,96,128]{4,3,2,1,0:T(8,128)(2,1)S(1)} %collective-permute-done.5.refs_2_), channel_id=1, source_target_pairs={{0,4},{4,8},{8,12},{12,16},{16,20},{20,24},{24,28},{28,32},{32,36}... | collective-permute-start | bytes 1769480 | tf_op jit(solution)/shard_map/ppermute | solution.py:123
  73.6 33.5 %collective-permute-start.14 = (bf16[2,4,3,96,128]{4,3,2,1,0:T(8,128)(2,1)}, bf16[2,4,3,96,128]{4,3,2,1,0:T(8,128)(2,1)}, u32[]{:S(2)}, u32[]{:S(2)}) collective-permute-start(bf16[2,4,3,96,128]{4,3,2,1,0:T(8,128)(2,1)} %collective-permute-done.13.refs_14_), channel_id=1, source_target_pairs={{0,60},{4,0},{8,4},{12,8},{16,12},{20,16},{24,20},{28,24},{32,28},... | collective-permute-start | bytes 1769480 | tf_op jit(solution)/shard_map/ppermute | solution.py:124
  88.3 23.8 %collective-permute-start.7 = (bf16[2,4,3,96,128]{4,3,2,1,0:T(8,128)(2,1)}, bf16[2,4,3,96,128]{4,3,2,1,0:T(8,128)(2,1)}, u32[]{:S(2)}, u32[]{:S(2)}) collective-permute-start(bf16[2,4,3,96,128]{4,3,2,1,0:T(8,128)(2,1)} %collective-permute-done.6.refs_3_), channel_id=1, source_target_pairs={{0,4},{4,8},{8,12},{12,16},{16,20},{20,24},{24,28},{28,32},{32,36}... | collective-permute-start | bytes 1769480 | tf_op jit(solution)/shard_map/ppermute | solution.py:123
  94.5 84.6 %copy-start.6 = (bf16[192,192]{1,0:T(8,128)(2,1)S(1)}, bf16[192,192]{1,0:T(8,128)(2,1)}, u32[]{:S(2)}) copy-start(bf16[192,192]{1,0:T(8,128)(2,1)} %constant.4.clone.to_sorted_ref) | copy-start | bytes 221188
  94.5 84.5 %all-to-all-start = ((bf16[32,24,2048]{2,1,0:T(8,128)(2,1)}), bf16[32,24,2048]{2,1,0:T(8,128)(2,1)S(1)}, u32[]{:S(2)}, u32[]{:S(2)}) async-start(bf16[32,24,2048]{2,1,0:T(8,128)(2,1)} %bitcast.12), calls=%async_computation | async-start | bytes 6291456 | tf_op jit(solution)/shard_map/all_to_all | solution.py:364
  107.2 17.6 %collective-permute-start.15 = (bf16[2,4,3,96,128]{4,3,2,1,0:T(8,128)(2,1)}, bf16[2,4,3,96,128]{4,3,2,1,0:T(8,128)(2,1)S(1)}, u32[]{:S(2)}, u32[]{:S(2)}) collective-permute-start(bf16[2,4,3,96,128]{4,3,2,1,0:T(8,128)(2,1)} %collective-permute-done.14.refs_13_), channel_id=1, source_target_pairs={{0,60},{4,0},{8,4},{12,8},{16,12},{20,16},{24,20},{28,24},{32,28},... | collective-permute-start | bytes 1769480 | tf_op jit(solution)/shard_map/ppermute | solution.py:124
  112.1 17.9 %collective-permute-start.8 = (bf16[2,4,3,96,128]{4,3,2,1,0:T(8,128)(2,1)}, bf16[2,4,3,96,128]{4,3,2,1,0:T(8,128)(2,1)S(1)}, u32[]{:S(2)}, u32[]{:S(2)}) collective-permute-start(bf16[2,4,3,96,128]{4,3,2,1,0:T(8,128)(2,1)} %collective-permute-done.7.refs_4_), channel_id=1, source_target_pairs={{0,4},{4,8},{8,12},{12,16},{16,20},{20,24},{24,28},{28,32},{32,36}... | collective-permute-start | bytes 1769480 | tf_op jit(solution)/shard_map/ppermute | solution.py:123
  124.8 16.8 %collective-permute-start.16 = (bf16[2,4,3,96,128]{4,3,2,1,0:T(8,128)(2,1)S(1)}, bf16[2,4,3,96,128]{4,3,2,1,0:T(8,128)(2,1)S(1)}, u32[]{:S(2)}, u32[]{:S(2)}) collective-permute-start(bf16[2,4,3,96,128]{4,3,2,1,0:T(8,128)(2,1)S(1)} %collective-permute-done.15.refs_12_), channel_id=1, source_target_pairs={{0,60},{4,0},{8,4},{12,8},{16,12},{20,16},{24,20},{28,24},{32,28},... | collective-permute-start | bytes 1769480 | tf_op jit(solution)/shard_map/ppermute | solution.py:124
  130.0 16.9 %collective-permute-start.9 = (bf16[2,4,3,96,128]{4,3,2,1,0:T(8,128)(2,1)S(1)}, bf16[2,4,3,96,128]{4,3,2,1,0:T(8,128)(2,1)S(1)}, u32[]{:S(2)}, u32[]{:S(2)}) collective-permute-start(bf16[2,4,3,96,128]{4,3,2,1,0:T(8,128)(2,1)S(1)} %collective-permute-done.8.refs_5_), channel_id=1, source_target_pairs={{0,4},{4,8},{8,12},{12,16},{16,20},{20,24},{24,28},{28,32},{32,36}... | collective-permute-start | bytes 1769480 | tf_op jit(solution)/shard_map/ppermute | solution.py:123
  141.6 16.0 %collective-permute-start.17 = (bf16[2,4,3,96,128]{4,3,2,1,0:T(8,128)(2,1)S(1)}, bf16[2,4,3,96,128]{4,3,2,1,0:T(8,128)(2,1)S(1)}, u32[]{:S(2)}, u32[]{:S(2)}) collective-permute-start(bf16[2,4,3,96,128]{4,3,2,1,0:T(8,128)(2,1)S(1)} %collective-permute-done.16.refs_11_), channel_id=1, source_target_pairs={{0,60},{4,0},{8,4},{12,8},{16,12},{20,16},{24,20},{28,24},{32,28},... | collective-permute-start | bytes 1769480 | tf_op jit(solution)/shard_map/ppermute | solution.py:124
  146.9 16.1 %collective-permute-start.10 = (bf16[2,4,3,96,128]{4,3,2,1,0:T(8,128)(2,1)S(1)}, bf16[2,4,3,96,128]{4,3,2,1,0:T(8,128)(2,1)S(1)}, u32[]{:S(2)}, u32[]{:S(2)}) collective-permute-start(bf16[2,4,3,96,128]{4,3,2,1,0:T(8,128)(2,1)S(1)} %collective-permute-done.9.refs_6_), channel_id=1, source_target_pairs={{0,4},{4,8},{8,12},{12,16},{16,20},{20,24},{24,28},{28,32},{32,36}... | collective-permute-start | bytes 1769480 | tf_op jit(solution)/shard_map/ppermute | solution.py:123
  157.6 15.2 %collective-permute-start.18 = (bf16[2,4,3,96,128]{4,3,2,1,0:T(8,128)(2,1)S(1)}, bf16[2,4,3,96,128]{4,3,2,1,0:T(8,128)(2,1)S(1)}, u32[]{:S(2)}, u32[]{:S(2)}) collective-permute-start(bf16[2,4,3,96,128]{4,3,2,1,0:T(8,128)(2,1)S(1)} %collective-permute-done.17.refs_10_), channel_id=1, source_target_pairs={{0,60},{4,0},{8,4},{12,8},{16,12},{20,16},{24,20},{28,24},{32,28},... | collective-permute-start | bytes 1769480 | tf_op jit(solution)/shard_map/ppermute | solution.py:124
  163.0 17.0 %collective-permute-start.11 = (bf16[4,3,96,128]{3,2,1,0:T(8,128)(2,1)S(1)}, bf16[4,3,96,128]{3,2,1,0:T(8,128)(2,1)}, u32[]{:S(2)}, u32[]{:S(2)}) collective-permute-start(bf16[4,3,96,128]{3,2,1,0:T(8,128)(2,1)S(1)} %slice_bitcast_fusion.1), channel_id=1, source_target_pairs={{0,4},{4,8},{8,12},{12,16},{16,20},{20,24},{24,28},{28,32},{32,36}... | collective-permute-start | bytes 884744 | tf_op jit(solution)/shard_map/ppermute | solution.py:125
  173.7 9.3 %collective-permute-start.19 = (bf16[4,3,96,128]{3,2,1,0:T(8,128)(2,1)}, bf16[4,3,96,128]{3,2,1,0:T(8,128)(2,1)}, u32[]{:S(2)}, u32[]{:S(2)}) collective-permute-start(bf16[4,3,96,128]{3,2,1,0:T(8,128)(2,1)} %slice_bitcast_fusion), channel_id=1, source_target_pairs={{0,60},{4,0},{8,4},{12,8},{16,12},{20,16},{24,20},{28,24},{32,28},... | collective-permute-start | bytes 884744 | tf_op jit(solution)/shard_map/ppermute | solution.py:126
  (20 other events, 535.1 us)
